TPU v7x, 32 devices: a whole 2x2x4 slice. The times are simulated.
32 devices in a mesh: row: 8 (over y, x, core), col: 4 (over z).
Axes of the slice: x: 2, y: 2, z: 4, core: 2. Of those that a mesh axis runs over, the one named last changes fastest.
Arguments:
- amplitudes: bfloat16 [256, 4096], P('row', 'col'), may hold values from -6 to 6
- integrals: bfloat16 [4096, 4096], P('col', 'row'), may hold values from -0.25 to 0.25
- occupied_irreps: int32 [256], replicated, may hold values from 0 to 7, as said below
- contracted_irreps: int32 [4096], P('col'), may hold values from 0 to 7
- output_irreps: int32 [4096], P('row'), may hold values from 0 to 7, as said below
Outputs:
- ladder: float32 [256, 4096], P('col', 'row')
Inputs may be any that keep to these rules, and one draw needn't show every extreme that they name: `occupied_irreps`: in each aligned block of 64 occupied pairs, every irrep appears exactly 64 // 8 times. `output_irreps`: in each aligned block of 512 output pairs, every irrep appears exactly 512 // 8 times.
All inputs are finite; a program needn't handle non-finite values.
Results may differ from a plain program's by a relative error of at most 0.0003.
Values may be sent and summed in bfloat16 or wider, within the bound.
No kernel may reach another device: no remote copies, remote signals or barrier semaphores. Data moves between devices by JAX's collectives and lax.ppermute only.
A program may use at most 64 MiB of HBM per device.

v0:
```python
import jax
import jax.numpy as jnp
from jax import lax
from jax.sharding import PartitionSpec as P


def body(amplitudes, integrals, occupied_irreps, contracted_irreps, output_irreps):
    col_count = lax.axis_size("col")
    pairs = occupied_irreps.shape[0]
    pair_share = pairs // col_count
    own_irreps = lax.dynamic_slice_in_dim(
        occupied_irreps, lax.axis_index("col") * pair_share, pair_share, 0
    )
    allowed = contracted_irreps[:, None] == output_irreps[None, :]
    masked = jnp.where(allowed, integrals, jnp.zeros_like(integrals))
    partial_sums = jnp.dot(
        lax.all_gather(amplitudes, "row", axis=0, tiled=True),
        masked,
        preferred_element_type=jnp.float32,
    )
    summed = lax.psum_scatter(partial_sums, "col", scatter_dimension=0, tiled=True)
    matches = own_irreps[:, None] == output_irreps[None, :]
    return jnp.where(matches, summed, jnp.zeros_like(summed))


def solution(mesh):
    return jax.shard_map(
        body,
        mesh=mesh,
        in_specs=(P("row", "col"), P("col", "row"), P(), P("col"), P("row")),
        out_specs=P("col", "row"),
        check_vma=False,
    )
```

profile of v0, /device:TPU:0, one launch (start us, length us, event | category | flops | bytes accessed | tf_op | source)
XLA Modules:
  0.0 52.0 jit_solution(14986923095626221347)
XLA Ops:
  6.5 0.0 reduce-scatter.4.cloned.1.call-start
  6.5 11.6 %all_gather.3 = bf16[256,1024]{1,0:T(8,128)(2,1)S(1)} all-gather(bf16[32,1024]{1,0:T(8,128)(2,1)} %param.5), channel_id=1, replica_groups=mesh['row'=8,'col'=4] {'row'}, dimensions={0}, use_global_device_ids=true | all-gather | bytes 589824 | tf_op jit(solution)/shard_map/all_gather | solution.py:17
  18.1 1.9 %convolution_bitcast_fusion = f32[256,512]{0,1:T(8,128)S(1)} fusion(bf16[256,1024]{1,0:T(8,128)(2,1)S(1)} %all_gather.3, bf16[1024,512]{1,0:T(8,128)(2,1)} %param.6, s32[512]{0:T(512)} %param.9, s32[1024]{0:T(1024)} %param.8), kind=kOutput, calls=%fused_computation.1 | convolution fusion | flops 269484032 | bytes 2103296 | tf_op jit(solution)/shard_map/dot_general | solution.py:16
  20.1 0.0 copy-start.1
  20.1 0.0 copy-start
  20.1 1.0 %copy.8 = f32[256,512]{1,0:T(8,128)} copy(f32[256,512]{0,1:T(8,128)S(1)} %convolution_bitcast_fusion) | data formatting | bytes 1048576
  21.1 0.0 reduce-scatter.4.cloned.1.call-update
  21.1 0.0 copy-done.1
  21.1 0.1 dynamic_slice.3
  21.2 22.0 %reduce-scatter.4.cloned.1.call-done = f32[64,512]{1,0:T(8,128)} async-done(((f32[256,512]{1,0:T(8,128)}), f32[64,512]{1,0:T(8,128)}) %reduce-scatter.4.cloned.1.call-update) | async-done | bytes 131088
  43.2 1.0 %copy.9 = f32[64,512]{0,1:T(8,128)S(1)} copy(f32[64,512]{1,0:T(8,128)} %reduce-scatter.4.cloned.1.call-done) | data formatting | bytes 262144
  44.2 0.0 copy-done
  44.2 0.1 compare_select_fusion.2
  44.4 0.8 %copy.7 = f32[64,512]{1,0:T(8,128)} copy(f32[64,512]{0,1:T(8,128)S(1)} %compare_select_fusion.2) | data formatting | bytes 262144 | tf_op jit(solution)/shard_map/jit(_where)/select_n | solution.py:23
Async XLA Ops:
  6.5 36.7 %reduce-scatter.4.cloned.1.call-start = ((), (), s32[]{:S(2)}) async-start(), calls=%async_computation.1 | async-start | bytes 655360
  20.1 1.1 %copy-start.1 = (s32[256]{0:T(256)S(1)}, s32[256]{0:T(256)}, u32[]{:S(2)}) copy-start(s32[256]{0:T(256)} %param.7) | copy-start | bytes 3076
  20.1 24.2 %copy-start = (s32[512]{0:T(512)S(1)}, s32[512]{0:T(512)}, u32[]{:S(2)}) copy-start(s32[512]{0:T(512)} %param.9) | copy-start | bytes 6148
Sparse Core Ops, SparseCore 0:
  21.2 21.9 reduce-scatter.3
where the time goes:
time: 52.2 us; the launch traced here: 52 us
  waiting for transfers between devices  22 us (42%)
  between operations  13.4 us (26%)
  blocking collectives  11.6 us (22%)
  local copies, waits for them, and re-layouts  2.88 us (6%)
  matrix products  1.93 us (4%)
    unnamed x2, waiting for transfers between devices  22 us
    all_gather x1, blocking collectives, body(): lax.all_gather(amplitudes, 'row', axis=0, tiled=True)  11.6 us
    unnamed x6, local copies, waits for them, and re-layouts  2.03 us
    dot_general x1, matrix products, body(): jnp.dot(lax.all_gather(amplitudes, 'row', axis=0, tiled=True), masked, pr...  1.93 us
  transfers between devices with their start and end apart: 1, of which 1 were waited for; matrix products, arithmetic and copies ran while one was open for 0% of the time, Pallas kernels for 0%

commit v1 on v0

--- a/solution.py
+++ b/solution.py
@@ -2,6 +2,31 @@
 import jax.numpy as jnp
 from jax import lax
 from jax.sharding import PartitionSpec as P
+
+
+def pools_take(block_here, in_dim=0):
+    all_rows = lax.axis_size("row")
+    mat_out, state_now, o_now = (all_rows, lax.axis_index("row"), block_here.shape[in_dim])
+    heap = [num * mat_out if i0 == in_dim else num for i0, num in enumerate(block_here.shape)]
+    y_new = lax.dynamic_update_slice_in_dim(
+        jnp.zeros(heap, block_here.dtype), block_here, state_now * o_now, axis=in_dim
+    )
+    z1 = kept_arr = block_here
+    src_i = 1
+    while src_i < mat_out // 2 + 1:
+        z1 = lax.ppermute(z1, "row", [(i0, (i0 + 1) % mat_out) for i0 in range(mat_out)])
+        y_new = lax.dynamic_update_slice_in_dim(
+            y_new, z1, (state_now - src_i) % mat_out * o_now, axis=in_dim
+        )
+        if 2 * src_i < mat_out:
+            kept_arr = lax.ppermute(
+                kept_arr, "row", [(i0, (i0 - 1) % mat_out) for i0 in range(mat_out)]
+            )
+            y_new = lax.dynamic_update_slice_in_dim(
+                y_new, kept_arr, (state_now + src_i) % mat_out * o_now, axis=in_dim
+            )
+        src_i += 1
+    return y_new
 
 
 def body(amplitudes, integrals, occupied_irreps, contracted_irreps, output_irreps):
@@ -13,11 +38,7 @@
     )
     allowed = contracted_irreps[:, None] == output_irreps[None, :]
     masked = jnp.where(allowed, integrals, jnp.zeros_like(integrals))
-    partial_sums = jnp.dot(
-        lax.all_gather(amplitudes, "row", axis=0, tiled=True),
-        masked,
-        preferred_element_type=jnp.float32,
-    )
+    partial_sums = jnp.dot(pools_take(amplitudes), masked, preferred_element_type=jnp.float32)
     summed = lax.psum_scatter(partial_sums, "col", scatter_dimension=0, tiled=True)
     matches = own_irreps[:, None] == output_irreps[None, :]
     return jnp.where(matches, summed, jnp.zeros_like(summed))

time: 52.2 us -> 59.5 us (1.14)
  blocking collectives: 11.6 us -> 0 us
  waiting for transfers between devices: 22 us -> 33 us
  starting transfers between devices: 0.01 us -> 8.72 us
  local copies, waits for them, and re-layouts: 2.88 us -> 1.07 us
  other arithmetic: 0.13 us -> 1.64 us
    reduce_scatter x0 -> x1, waiting for transfers between devices: none -> 23.4 us  [body(): lax.psum_scatter(partial_sums, 'col', scatter_dimension=0, tiled=True)]
    unnamed x2 -> x1, waiting for transfers between devices: 22 us -> 0.02 us
    all_gather x1 -> x0, blocking collectives: 11.6 us -> none  [body(): lax.all_gather(amplitudes, 'row', axis=0, tiled=True)]
    ppermute x0 -> x7, waiting for transfers between devices: none -> 9.57 us  [the longest x4 9.43 us: pools_take(): lax.ppermute(z1, 'row', [(i0, (i0 + 1) % mat_out) for i0 in range(mat_out)])]
    ppermute x0 -> x7, starting transfers between devices: none -> 8.72 us  [the longest x3 8.21 us: pools_take(): lax.ppermute(kept_arr, 'row', [(i0, (i0 - 1) % mat_out) for i0 in range(m...]
    unnamed x6 -> x8, local copies, waits for them, and re-layouts: 2.03 us -> 0.02 us
    select_n x1, other arithmetic: 0.13 us -> 1.64 us  [body(): return jnp.where(matches, summed, jnp.zeros_like(summed))]
    dynamic_update_slice x0 -> x8, local copies, waits for them, and re-layouts: none -> 0.93 us  [the longest x1 0.86 us: pools_take(): lax.dynamic_update_slice_in_dim(jnp.zeros(heap, block_here.dtype), block_...]
  transfers between devices with their start and end apart: 1 -> 8, of which waited for: 1 -> 6; matrix products, arithmetic and copies ran while one was open for 0% -> 2% of each run, Pallas kernels for 0% -> 0%
where the time goes in v1:
time: 59.5 us; the launch traced here: 59.3 us
  waiting for transfers between devices  33 us (55%)
  between operations  13.5 us (23%)
  starting transfers between devices  8.72 us (15%)
  other arithmetic  1.64 us (3%)
  matrix products  1.36 us (2%)
  local copies, waits for them, and re-layouts  1.07 us (2%)
    reduce_scatter x1, waiting for transfers between devices, body(): lax.psum_scatter(partial_sums, 'col', scatter_dimension=0, tiled=True)  23.4 us
    ppermute x4, waiting for transfers between devices, pools_take(): lax.ppermute(z1, 'row', [(i0, (i0 + 1) % mat_out) for i0 in range(mat_out)])  9.43 us
    ppermute x3, starting transfers between devices, pools_take(): lax.ppermute(kept_arr, 'row', [(i0, (i0 - 1) % mat_out) for i0 in range(m...  8.21 us
    select_n x1, other arithmetic, body(): return jnp.where(matches, summed, jnp.zeros_like(summed))  1.64 us
    dot_general x1, matrix products, body(): jnp.dot(pools_take(amplitudes), masked, preferred_element_type=jnp.float32)  1.36 us
  transfers between devices with their start and end apart: 8, of which 6 were waited for; matrix products, arithmetic and copies ran while one was open for 2% of the time, Pallas kernels for 0%

profile of v1, /device:TPU:0, one launch (start us, length us, event | category | flops | bytes accessed | tf_op | source)
XLA Modules:
  0.0 59.3 jit_solution(6653348136838585092)
XLA Ops:
  6.5 0.0 copy-start.1
  6.5 0.0 copy-start.2
  6.5 0.0 copy-start
  6.5 0.0 reduce-scatter.2.cloned.1.call-start
  6.5 0.5 collective-permute-start
  7.0 2.9 %collective-permute-start.1 = (bf16[32,1024]{1,0:T(8,128)(2,1)}, bf16[32,1024]{1,0:T(8,128)(2,1)S(1)}, u32[]{:S(2)}, u32[]{:S(2)}) collective-permute-start(bf16[32,1024]{1,0:T(8,128)(2,1)} %param.5), channel_id=1, source_target_pairs={{0,28},{4,0},{8,4},{12,8},{16,12},{20,16},{24,20},{28,24},{1,29},{... | collective-permute-start | bytes 196616 | tf_op jit(solution)/shard_map/ppermute | solution.py:22
  10.0 0.1 broadcast_in_dim.6
  10.1 0.9 %constant_dynamic-update-slice_fusion.7 = bf16[256,1024]{1,0:T(8,128)(2,1)S(1)} fusion(bf16[256,1024]{1,0:T(8,128)(2,1)S(1)} %broadcast_in_dim.6, bf16[32,1024]{1,0:T(8,128)(2,1)} %param.5, s32[]{:T(128)S(6)} %select_n.67), kind=kLoop, calls=%fused_computation.13 | loop fusion | bytes 131076 | tf_op jit(solution)/shard_map/dynamic_update_slice | solution.py:11
  10.9 1.2 %collective-permute-done = bf16[32,1024]{1,0:T(8,128)(2,1)S(1)} collective-permute-done((bf16[32,1024]{1,0:T(8,128)(2,1)}, bf16[32,1024]{1,0:T(8,128)(2,1)S(1)}, u32[]{:S(2)}, u32[]{:S(2)}) %collective-permute-start) | collective-permute-done | bytes 65568 | tf_op jit(solution)/shard_map/ppermute | solution.py:17
  12.1 0.0 collective-permute-start.2
  12.1 0.1 collective-permute-done.1
  12.2 2.6 %collective-permute-start.3 = (bf16[32,1024]{1,0:T(8,128)(2,1)S(1)}, bf16[32,1024]{1,0:T(8,128)(2,1)S(1)}, u32[]{:S(2)}, u32[]{:S(2)}) collective-permute-start(bf16[32,1024]{1,0:T(8,128)(2,1)S(1)} %collective-permute-done.1), channel_id=1, source_target_pairs={{0,28},{4,0},{8,4},{12,8},{16,12},{20,16},{24,20},{28,24},{1,29},{... | collective-permute-start | bytes 196616 | tf_op jit(solution)/shard_map/ppermute | solution.py:22
  14.8 1.9 %collective-permute-done.2 = bf16[32,1024]{1,0:T(8,128)(2,1)S(1)} collective-permute-done((bf16[32,1024]{1,0:T(8,128)(2,1)S(1)}, bf16[32,1024]{1,0:T(8,128)(2,1)S(1)}, u32[]{:S(2)}, u32[]{:S(2)}) %collective-permute-start.2) | collective-permute-done | bytes 65568 | tf_op jit(solution)/shard_map/ppermute | solution.py:17
  16.7 0.0 collective-permute-start.4
  16.7 0.0 collective-permute-done.3
  16.7 2.7 %collective-permute-start.5 = (bf16[32,1024]{1,0:T(8,128)(2,1)S(1)}, bf16[32,1024]{1,0:T(8,128)(2,1)S(1)}, u32[]{:S(2)}, u32[]{:S(2)}) collective-permute-start(bf16[32,1024]{1,0:T(8,128)(2,1)S(1)} %collective-permute-done.3), channel_id=1, source_target_pairs={{0,28},{4,0},{8,4},{12,8},{16,12},{20,16},{24,20},{28,24},{1,29},{... | collective-permute-start | bytes 196616 | tf_op jit(solution)/shard_map/ppermute | solution.py:22
  19.4 1.9 %collective-permute-done.4 = bf16[32,1024]{1,0:T(8,128)(2,1)S(1)} collective-permute-done((bf16[32,1024]{1,0:T(8,128)(2,1)S(1)}, bf16[32,1024]{1,0:T(8,128)(2,1)S(1)}, u32[]{:S(2)}, u32[]{:S(2)}) %collective-permute-start.4) | collective-permute-done | bytes 65568 | tf_op jit(solution)/shard_map/ppermute | solution.py:17
  21.3 0.0 collective-permute-start.6
  21.3 0.0 collective-permute-done.5
  21.3 4.5 %collective-permute-done.6 = bf16[32,1024]{1,0:T(8,128)(2,1)S(1)} collective-permute-done((bf16[32,1024]{1,0:T(8,128)(2,1)S(1)}, bf16[32,1024]{1,0:T(8,128)(2,1)S(1)}, u32[]{:S(2)}, u32[]{:S(2)}) %collective-permute-start.6) | collective-permute-done | bytes 65568 | tf_op jit(solution)/shard_map/ppermute | solution.py:17
  25.9 0.0 copy-done.1
  25.9 0.0 copy-done.2
  25.9 0.0 copy-done
  25.9 0.0 copy-start.3
  25.9 1.4 %fusion = f32[256,512]{1,0:T(8,128)} fusion(bf16[256,1024]{1,0:T(8,128)(2,1)S(1)} %constant_dynamic-update-slice_fusion, bf16[1024,512]{1,0:T(8,128)(2,1)S(1)} %copy-done.1, s32[512]{0:T(512)S(1)} %copy-done, s32[1024]{0:T(1024)S(1)} %copy-done.2), kind=kOutput, calls=%fused_computation.1 | convolution fusion | flops 269484032 | bytes 2103296 | tf_op jit(solution)/shard_map/dot_general | solution.py:41
  27.3 0.0 reduce-scatter.2.cloned.1.call-update
  27.3 0.0 copy-done.3
  27.3 0.1 dynamic_slice.3
  27.4 23.4 %reduce-scatter.2.cloned.1.call-done = f32[64,512]{1,0:T(8,128)} async-done(((f32[256,512]{1,0:T(8,128)}), f32[64,512]{1,0:T(8,128)}) %reduce-scatter.2.cloned.1.call-update) | async-done | bytes 131088 | tf_op jit(solution)/shard_map/reduce_scatter | solution.py:42
  50.8 1.6 %compare_select_fusion.2 = f32[64,512]{1,0:T(8,128)} fusion(f32[64,512]{1,0:T(8,128)} %reduce-scatter.2.cloned.1.call-done, s32[512]{0:T(512)S(1)} %copy-done, s32[64]{0:T(128)S(1)} %dynamic_slice.3), kind=kLoop, calls=%fused_computation.5 | loop fusion | flops 65536 | bytes 264448 | tf_op jit(solution)/shard_map/jit(_where)/select_n | solution.py:44
  (7 shorter events, 0.1 us)
Async XLA Ops:
  6.5 19.3 %copy-start.1 = (bf16[1024,512]{1,0:T(8,128)(2,1)S(1)}, bf16[1024,512]{1,0:T(8,128)(2,1)}, u32[]{:S(2)}) copy-start(bf16[1024,512]{1,0:T(8,128)(2,1)} %param.6) | copy-start | bytes 3145732
  6.5 19.3 %copy-start.2 = (s32[1024]{0:T(1024)S(1)}, s32[1024]{0:T(1024)}, u32[]{:S(2)}) copy-start(s32[1024]{0:T(1024)} %param.8) | copy-start | bytes 12292
  6.5 19.4 %copy-start = (s32[512]{0:T(512)S(1)}, s32[512]{0:T(512)}, u32[]{:S(2)}) copy-start(s32[512]{0:T(512)} %param.9) | copy-start | bytes 6148
  6.5 44.3 %reduce-scatter.2.cloned.1.call-start = ((), (), s32[]{:S(2)}) async-start(), calls=%async_computation.1 | async-start | bytes 655360 | tf_op jit(solution)/shard_map/reduce_scatter | solution.py:42
  6.5 5.5 %collective-permute-start = (bf16[32,1024]{1,0:T(8,128)(2,1)}, bf16[32,1024]{1,0:T(8,128)(2,1)S(1)}, u32[]{:S(2)}, u32[]{:S(2)}) collective-permute-start(bf16[32,1024]{1,0:T(8,128)(2,1)} %param.5), channel_id=1, source_target_pairs={{0,4},{4,8},{8,12},{12,16},{16,20},{20,24},{24,28},{28,0},{1,5},{5... | collective-permute-start | bytes 196616 | tf_op jit(solution)/shard_map/ppermute | solution.py:17
  7.0 5.2 %collective-permute-start.1 = (bf16[32,1024]{1,0:T(8,128)(2,1)}, bf16[32,1024]{1,0:T(8,128)(2,1)S(1)}, u32[]{:S(2)}, u32[]{:S(2)}) collective-permute-start(bf16[32,1024]{1,0:T(8,128)(2,1)} %param.5), channel_id=1, source_target_pairs={{0,28},{4,0},{8,4},{12,8},{16,12},{20,16},{24,20},{28,24},{1,29},{... | collective-permute-start | bytes 196616 | tf_op jit(solution)/shard_map/ppermute | solution.py:22
  12.1 4.6 %collective-permute-start.2 = (bf16[32,1024]{1,0:T(8,128)(2,1)S(1)}, bf16[32,1024]{1,0:T(8,128)(2,1)S(1)}, u32[]{:S(2)}, u32[]{:S(2)}) collective-permute-start(bf16[32,1024]{1,0:T(8,128)(2,1)S(1)} %collective-permute-done), channel_id=1, source_target_pairs={{0,4},{4,8},{8,12},{12,16},{16,20},{20,24},{24,28},{28,0},{1,5},{5... | collective-permute-start | bytes 196616 | tf_op jit(solution)/shard_map/ppermute | solution.py:17
  12.2 4.5 %collective-permute-start.3 = (bf16[32,1024]{1,0:T(8,128)(2,1)S(1)}, bf16[32,1024]{1,0:T(8,128)(2,1)S(1)}, u32[]{:S(2)}, u32[]{:S(2)}) collective-permute-start(bf16[32,1024]{1,0:T(8,128)(2,1)S(1)} %collective-permute-done.1), channel_id=1, source_target_pairs={{0,28},{4,0},{8,4},{12,8},{16,12},{20,16},{24,20},{28,24},{1,29},{... | collective-permute-start | bytes 196616 | tf_op jit(solution)/shard_map/ppermute | solution.py:22
  16.7 4.6 %collective-permute-start.4 = (bf16[32,1024]{1,0:T(8,128)(2,1)S(1)}, bf16[32,1024]{1,0:T(8,128)(2,1)S(1)}, u32[]{:S(2)}, u32[]{:S(2)}) collective-permute-start(bf16[32,1024]{1,0:T(8,128)(2,1)S(1)} %collective-permute-done.2), channel_id=1, source_target_pairs={{0,4},{4,8},{8,12},{12,16},{16,20},{20,24},{24,28},{28,0},{1,5},{5... | collective-permute-start | bytes 196616 | tf_op jit(solution)/shard_map/ppermute | solution.py:17
  16.7 4.6 %collective-permute-start.5 = (bf16[32,1024]{1,0:T(8,128)(2,1)S(1)}, bf16[32,1024]{1,0:T(8,128)(2,1)S(1)}, u32[]{:S(2)}, u32[]{:S(2)}) collective-permute-start(bf16[32,1024]{1,0:T(8,128)(2,1)S(1)} %collective-permute-done.3), channel_id=1, source_target_pairs={{0,28},{4,0},{8,4},{12,8},{16,12},{20,16},{24,20},{28,24},{1,29},{... | collective-permute-start | bytes 196616 | tf_op jit(solution)/shard_map/ppermute | solution.py:22
  21.3 4.6 %collective-permute-start.6 = (bf16[32,1024]{1,0:T(8,128)(2,1)S(1)}, bf16[32,1024]{1,0:T(8,128)(2,1)S(1)}, u32[]{:S(2)}, u32[]{:S(2)}) collective-permute-start(bf16[32,1024]{1,0:T(8,128)(2,1)S(1)} %collective-permute-done.4), channel_id=1, source_target_pairs={{0,4},{4,8},{8,12},{12,16},{16,20},{20,24},{24,28},{28,0},{1,5},{5... | collective-permute-start | bytes 196616 | tf_op jit(solution)/shard_map/ppermute | solution.py:17
  25.9 1.4 %copy-start.3 = (s32[256]{0:T(256)S(1)}, s32[256]{0:T(256)}, u32[]{:S(2)}) copy-start(s32[256]{0:T(256)} %param.7) | copy-start | bytes 3076
Sparse Core Ops, SparseCore 0:
  27.4 23.3 reduce-scatter.1
